TPU v7x, 512 devices: a whole 4x8x8 slice. The times are simulated.
512 devices in a mesh: dp: 16 (over z, core), tp: 32 (over y, x).
Axes of the slice: x: 4, y: 8, z: 8, core: 2. Of those that a mesh axis runs over, the one named last changes fastest.
Arguments:
- q_new: bfloat16 [512, 1536], P(('dp', 'tp'))
- new_key_value: bfloat16 [512, 512], P(('dp', 'tp')), may hold values from -6 to 6
- resid_dec: bfloat16 [512, 1536], P(('dp', 'tp')), may hold values from -6 to 6
- placing: int32 [512], replicated, may hold values from 0 to 511, as said below
- lengths: int32 [512], P('dp'), may hold values from 5 to 2048, as said below
- write_pos: int32 [512], P('dp'), may hold values from 4 to 2047, as said below
- k_cache: bfloat16 [512, 2, 2048, 128], P('dp', None, 'tp')
- value_cache: bfloat16 [512, 2, 2048, 128], P('dp', None, 'tp'), may hold values from -6 to 6
- w_out: bfloat16 [1536, 1536], P(None, 'tp'), may hold values from -0.15625 to 0.15625
- x_pre: bfloat16 [32256, 1536], P(('dp', 'tp')), may hold values from -6 to 6
- routes: int32 [32768, 4], P(('dp', 'tp')), may hold values from 0 to 31, all different within a row; in each aligned block of 64 rows (0 to 63, 64 to 127, ...) at most 16 rows name the same one
- route_scale: float32 [32768, 4], P(('dp', 'tp')), may hold values from 0.2 to 2
- moe_gain: float32 [1536], replicated, may hold values from 0.5 to 1.5
- w_gate: bfloat16 [32, 768, 1536], P('tp', 'dp'), may hold values from -0.15625 to 0.15625
- w_up: bfloat16 [32, 768, 1536], P('tp', 'dp'), may hold values from -0.15625 to 0.15625
- w_down: bfloat16 [32, 768, 1536], P('tp', 'dp'), may hold values from -0.21875 to 0.21875
Outputs:
- out_pre: bfloat16 [32256, 1536], P(('dp', 'tp'))
- out_dec: bfloat16 [512, 1536], P(('dp', 'tp'))
Inputs may be any that keep to these rules, and one draw needn't show every extreme that they name: Each of 0 to 511 appears once; cache row j belongs to request placing[j]. `lengths`: a cache row is either full (2048 live slots) or filled from slot 0 up; some row is full. `write_pos`: below the row's length; a row that is not full writes at its length - 1, a full row anywhere past the sink slots. `routes`: the 64 rows of one device name any one expert at most 16 times.
All inputs are finite; a program needn't handle non-finite values.
Results may differ from a plain program's by a relative error of at most 0.007.
Values may be sent and summed in bfloat16 or wider, within the bound.
No kernel may reach another device: no remote copies, remote signals or barrier semaphores. Data moves between devices by JAX's collectives and lax.ppermute only.
A program may use at most 64 MiB of HBM per device.

v0:
```python
import jax
import jax.numpy as jnp
from jax import lax
from jax.sharding import PartitionSpec as P

HIGHEST = lax.Precision.HIGHEST


def contract_rows(left_rows, unit_rows):
    return lax.dot_general(
        left_rows, unit_rows, (((1,), (1,)), ((), ())), preferred_element_type=jnp.float32
    )


def on_device(
    q_new,
    new_key_value,
    resid_dec,
    placing,
    lengths,
    write_pos,
    k_cache,
    value_cache,
    w_out,
    x_pre,
    routes,
    route_scale,
    moe_gain,
    w_gate,
    w_up,
    w_down,
):
    tp_size = lax.axis_size("tp")
    dp_group = lax.axis_index("dp")
    tp_lane = lax.axis_index("tp")
    group_reqs = k_cache.shape[0]
    kv_heads = k_cache.shape[1]
    slot_dev = k_cache.shape[2]
    head_size = k_cache.shape[3]
    query_width = q_new.shape[1]
    per_group = query_width // head_size // kv_heads
    fetched = (
        lax.all_gather(w_gate, "dp", axis=1, tiled=True),
        lax.all_gather(w_up, "dp", axis=1, tiled=True),
        lax.all_gather(w_down, "dp", axis=1, tiled=True),
    )
    all_query, all_new = (
        lax.all_gather(q_new, ("dp", "tp"), axis=0, tiled=True),
        lax.all_gather(new_key_value, ("dp", "tp"), axis=0, tiled=True),
    )
    my_rows = lax.dynamic_slice_in_dim(placing, dp_group * group_reqs, group_reqs)
    query_rows = jnp.take(all_query, my_rows, axis=0)
    fresh_rows = jnp.take(all_new, my_rows, axis=0)
    slot_ids = tp_lane * slot_dev + jnp.arange(slot_dev, dtype=jnp.int32)
    incoming_key = fresh_rows[:, : kv_heads * head_size].reshape(group_reqs, kv_heads, 1, head_size)
    incoming_value = fresh_rows[:, kv_heads * head_size :].reshape(
        group_reqs, kv_heads, 1, head_size
    )
    written = (slot_ids[None, :] == write_pos[:, None])[:, None, :, None]
    key_rows = jnp.where(written, incoming_key, k_cache)
    value_rows = jnp.where(written, incoming_value, value_cache).astype(jnp.float32)
    query_head_list = query_rows.reshape(group_reqs, kv_heads, per_group, head_size)
    scores = jnp.einsum(
        "rgqd,rgsd->rgqs", query_head_list, key_rows, preferred_element_type=jnp.float32
    ) * head_size ** (-0.5)
    is_valid = (slot_ids[None, :] < lengths[:, None])[:, None, None, :]
    masked = jnp.where(is_valid, scores, -1e30)
    local_peak = jnp.max(masked, axis=-1)
    peak = lax.pmax(local_peak, "tp")
    weights = jnp.where(is_valid, jnp.exp(masked - peak[..., None]), 0.0)
    local_total = jnp.sum(weights, axis=-1)
    local_mixed = jnp.einsum("rgqs,rgsd->rgqd", weights, value_rows, precision=HIGHEST)
    weight_total, mixed_sum = lax.psum((local_total, local_mixed), "tp")
    attention = (
        (mixed_sum / weight_total[..., None]).reshape(group_reqs, query_width).astype(jnp.bfloat16)
    )
    projected = jnp.dot(attention, w_out, preferred_element_type=jnp.float32).astype(jnp.bfloat16)
    cache_row = lax.all_to_all(projected, "tp", split_axis=0, concat_axis=1, tiled=True)
    all_proj = lax.all_gather(cache_row, ("dp", "tp"), axis=0, tiled=True)
    total_reqs = placing.shape[0]
    my_request = dp_group * tp_size + tp_lane
    where_cached = jnp.sum(
        jnp.where(placing == my_request, jnp.arange(total_reqs, dtype=jnp.int32), 0)
    )
    proj_home = lax.dynamic_slice_in_dim(all_proj, where_cached, 1, 0)
    hidden_dec = (resid_dec.astype(jnp.float32) + proj_home.astype(jnp.float32)).astype(
        jnp.bfloat16
    )
    moe_rows = jnp.concatenate([x_pre, hidden_dec], axis=0)
    rows_dev = moe_rows.shape[0]
    width = moe_rows.shape[1]
    top_count = routes.shape[1]
    experts = tp_size * w_gate.shape[0]
    capacity = min(2 * rows_dev * top_count // experts, rows_dev)
    rows_f32 = moe_rows.astype(jnp.float32)
    mean_square = jnp.mean(rows_f32 * rows_f32, axis=-1, keepdims=True)
    normed = (rows_f32 * lax.rsqrt(mean_square + 1e-06) * moe_gain).astype(jnp.bfloat16)
    route_weight = route_scale / jnp.sum(route_scale, axis=-1, keepdims=True)
    expert_ids = routes.reshape(rows_dev * top_count)
    onehot = (expert_ids[:, None] == jnp.arange(experts, dtype=jnp.int32)[None, :]).astype(
        jnp.int32
    )
    position = jnp.sum(onehot * (jnp.cumsum(onehot, axis=0) - onehot), axis=-1)
    slot_index = expert_ids * capacity + position
    slot_rows = slot_index.reshape(rows_dev, top_count)
    pick_table = jnp.any(
        slot_rows[:, :, None] == jnp.arange(experts * capacity, dtype=jnp.int32)[None, None, :],
        axis=1,
    ).astype(jnp.bfloat16)
    outgoing = jnp.einsum(
        "rc,rd->cd", pick_table, normed, preferred_element_type=jnp.float32
    ).astype(jnp.bfloat16)
    outgoing = outgoing.reshape(experts, capacity, width)
    received = lax.all_to_all(outgoing, "tp", split_axis=0, concat_axis=0, tiled=True)
    flat_rows = received.reshape(-1, received.shape[-1])
    gate = contract_rows(flat_rows, fetched[0][0])
    upper = contract_rows(flat_rows, fetched[1][0])
    active = (jnp.maximum(gate, 0.0) * upper).astype(jnp.bfloat16)
    output = jnp.dot(active, fetched[2][0], preferred_element_type=jnp.float32)
    expert_out = output.astype(jnp.bfloat16).reshape(received.shape)
    returned = lax.all_to_all(expert_out, "tp", split_axis=0, concat_axis=0, tiled=True)
    flat_back = returned.reshape(experts * capacity, width)
    picked = jnp.take(flat_back, slot_index, axis=0).reshape(rows_dev, top_count, width)
    mixture = jnp.sum(route_weight[:, :, None] * picked.astype(jnp.float32), axis=1)
    moe_out = (rows_f32 + mixture).astype(jnp.bfloat16)
    return (moe_out[: rows_dev - 1], moe_out[rows_dev - 1 :])


def solution(mesh):
    placed = (
        P(("dp", "tp"), None),
        P(("dp", "tp"), None),
        P(("dp", "tp"), None),
        P(),
        P("dp"),
        P("dp"),
        P("dp", None, "tp", None),
        P("dp", None, "tp", None),
        P(None, "tp"),
        P(("dp", "tp"), None),
        P(("dp", "tp"), None),
        P(("dp", "tp"), None),
        P(),
        P("tp", "dp", None),
        P("tp", "dp", None),
        P("tp", "dp", None),
    )
    return jax.shard_map(
        on_device,
        mesh=mesh,
        in_specs=placed,
        out_specs=(P(("dp", "tp"), None), P(("dp", "tp"), None)),
        check_vma=False,
    )
```

profile of v0, /device:TPU:4, one launch (start us, length us, event | category | flops | bytes accessed | tf_op | source)
XLA Modules:
  0.0 762.3 jit_solution(4975138523507420202)
XLA Ops:
  8.0 132.2 %all-gather.1 = bf16[512,1,512]{2,1,0:T(2,128)(2,1)S(1)} all-gather(bf16[1,1,512]{2,1,0:T(2,128)(2,1)} %bitcast.66), channel_id=1, replica_groups=mesh['dp'=16,'tp'=32] {'dp','tp'}, dimensions={0}, use_global_device_ids=true | all-gather | bytes 525312 | tf_op jit(solution)/shard_map/all_gather | solution.py:49
  141.3 2.3 copy.59
  144.4 1.1 fusion.45
  145.6 138.1 %pmax.7 = f32[32,2,6]{2,1,0:T(2,128)S(1)} all-reduce(f32[32,2,6]{2,1,0:T(2,128)S(1)} %get-tuple-element.10), channel_id=1, replica_groups=mesh['dp'=16,'tp'=32] {'tp'}, use_global_device_ids=true, to_apply=%region_1.2 | all-reduce | flops 384 | bytes 3072 | tf_op jit(solution)/shard_map/pmax | solution.py:69
  283.7 1.9 fusion.9
  286.0 137.7 %psum.15 = f32[32,2,6]{2,1,0:T(2,128)S(1)} all-reduce(f32[32,2,6]{2,1,0:T(2,128)S(1)} %fusion.23), channel_id=1, replica_groups=mesh['dp'=16,'tp'=32] {'tp'}, use_global_device_ids=true, to_apply=%region_4.5 | all-reduce | flops 384 | bytes 3072 | tf_op jit(solution)/shard_map/psum | solution.py:73
  423.7 13.1 %all-reduce.2.cloned.1.call-done = f32[32,2,6,128]{3,2,1,0:T(8,128)} async-done(((f32[32,2,6,128]{3,2,1,0:T(8,128)}), f32[32,2,6,128]{3,2,1,0:T(8,128)}) %all-reduce.2.cloned.1.call-update) | async-done | bytes 196624 | tf_op jit(solution)/shard_map/psum | solution.py:73
  436.8 1.1 divide_convert_fusion
  438.2 14.8 %all_to_all.26 = bf16[32,1,48]{2,1,0:T(2,128)(2,1)S(1)} all-to-all(bf16[32,1,48]{2,1,0:T(2,128)(2,1)S(1)} %copy.45), channel_id=1, replica_groups=mesh['dp'=16,'tp'=32] {'tp'}, dimensions={0} | all-to-all | bytes 6144 | tf_op jit(solution)/shard_map/all_to_all | solution.py:78
  453.1 0.7 reshape.210
  459.7 107.4 %all-gather.17.cloned.1.call-done = bf16[512,1,1536]{2,1,0:T(2,128)(2,1)} async-done(((bf16[1,1,1536]{2,1,0:T(2,128)(2,1)}), bf16[512,1,1536]{2,1,0:T(2,128)(2,1)}) %all-gather.17.cloned.1.call-update) | async-done | bytes 1572880 | tf_op jit(solution)/shard_map/all_gather | solution.py:79
  567.1 0.7 fusion.37
  568.0 1.8 convolution_convert_fusion.1
  569.8 7.1 all-to-all-start.1
  576.9 31.7 %all-gather.11.cloned.1.call-done = bf16[1,768,1536]{2,1,0:T(8,128)(2,1)} async-done(((bf16[1,48,1536]{2,1,0:T(8,128)(2,1)}), bf16[1,768,1536]{2,1,0:T(8,128)(2,1)}) %all-gather.11.cloned.1.call-update) | async-done | bytes 2359312 | tf_op jit(solution)/shard_map/all_gather | solution.py:44
  608.6 8.0 %all-to-all-done.1 = bf16[32,16,1536]{2,1,0:T(8,128)(2,1)S(1)} async-done(((bf16[32,16,1536]{2,1,0:T(8,128)(2,1)}), bf16[32,16,1536]{2,1,0:T(8,128)(2,1)S(1)}, u32[]{:S(2)}, u32[]{:S(2)}) %all-to-all-start.1) | async-done | bytes 1572896 | tf_op jit(solution)/shard_map/all_to_all | solution.py:114
  616.6 3.1 fusion.1
  619.7 32.1 %all-gather.13.cloned.1.call-done = bf16[1,768,1536]{2,1,0:T(8,128)(2,1)} async-done(((bf16[1,48,1536]{2,1,0:T(8,128)(2,1)}), bf16[1,768,1536]{2,1,0:T(8,128)(2,1)}) %all-gather.13.cloned.1.call-update) | async-done | bytes 2359312 | tf_op jit(solution)/shard_map/all_gather | solution.py:45
  651.9 43.5 %all-gather.9.cloned.1.call-done = bf16[1,768,1536]{2,1,0:T(8,128)(2,1)} async-done(((bf16[1,48,1536]{2,1,0:T(8,128)(2,1)}), bf16[1,768,1536]{2,1,0:T(8,128)(2,1)}) %all-gather.9.cloned.1.call-update) | async-done | bytes 2359312 | tf_op jit(solution)/shard_map/all_gather | solution.py:43
  695.4 6.7 convolution_convert_fusion
  702.1 10.0 %all-to-all-start.2 = ((bf16[32,16,1536]{2,1,0:T(8,128)(2,1)}), bf16[32,16,1536]{2,1,0:T(8,128)(2,1)S(1)}, u32[]{:S(2)}, u32[]{:S(2)}) async-start(bf16[32,16,1536]{2,1,0:T(8,128)(2,1)} %bitcast.10), calls=%async_computation.2 | async-start | bytes 3145728 | tf_op jit(solution)/shard_map/all_to_all | solution.py:121
  712.6 39.2 %all-to-all-done.2 = bf16[32,16,1536]{2,1,0:T(8,128)(2,1)S(1)} async-done(((bf16[32,16,1536]{2,1,0:T(8,128)(2,1)}), bf16[32,16,1536]{2,1,0:T(8,128)(2,1)S(1)}, u32[]{:S(2)}, u32[]{:S(2)}) %all-to-all-start.2) | async-done | bytes 1572896 | tf_op jit(solution)/shard_map/all_to_all | solution.py:121
  751.8 1.3 gather_fusion.2
  753.2 1.5 multiply_reduce_fusion
  (82 shorter events, 8.8 us)
Async XLA Ops:
  7.2 430.9 %copy-start = (bf16[1536,48]{0,1:T(8,128)(2,1)S(1)}, bf16[1536,48]{0,1:T(8,128)(2,1)}, u32[]{:S(2)}) copy-start(bf16[1536,48]{0,1:T(8,128)(2,1)} %param.24) | copy-start | bytes 442372
  7.2 133.2 %copy-start.7 = (s32[512]{0:T(512)S(1)}, s32[512]{0:T(512)}, u32[]{:S(2)}) copy-start(s32[512]{0:T(512)} %param.19) | copy-start | bytes 6148
  7.2 134.1 %all-gather.15.cloned.1.call-start = ((), (), s32[]{:S(2)}) async-start(), calls=%async_computation.7 | async-start | bytes 3151872 | tf_op jit(solution)/shard_map/all_gather | solution.py:48
  7.9 428.9 %all-reduce.2.cloned.1.call-start = ((), (), s32[]{:S(2)}) async-start(), calls=%async_computation.3 | async-start | bytes 524288 | tf_op jit(solution)/shard_map/psum | solution.py:73
  8.0 133.2 %copy-start.8 = (s32[32]{0:T(128)S(1)}, s32[32]{0:T(128)}, u32[]{:S(2)}) copy-start(s32[32]{0:T(128)} %param.20) | copy-start | bytes 388
  8.0 133.2 %copy-start.9 = (s32[32]{0:T(128)S(1)}, s32[32]{0:T(128)}, u32[]{:S(2)}) copy-start(s32[32]{0:T(128)} %param.21) | copy-start | bytes 388
  141.3 3.1 copy-start.10
  144.3 139.4 %copy-start.11 = (bf16[32,2,64,128]{3,2,1,0:T(8,128)(2,1)S(1)}, bf16[32,2,64,128]{3,2,1,0:T(8,128)(2,1)}, u32[]{:S(2)}) copy-start(bf16[32,2,64,128]{3,2,1,0:T(8,128)(2,1)} %param.23) | copy-start | bytes 3145732
  285.6 169.9 %copy-start.3 = (s32[64,4]{0,1:T(4,128)S(1)}, s32[64,4]{0,1:T(4,128)}, u32[]{:S(2)}) copy-start(s32[64,4]{0,1:T(4,128)} %param.26) | copy-start | bytes 3076
  285.6 281.5 %copy-start.6 = (bf16[1,1536]{1,0:T(2,128)(2,1)S(1)}, bf16[1,1536]{1,0:T(2,128)(2,1)}, u32[]{:S(2)}) copy-start(bf16[1,1536]{1,0:T(2,128)(2,1)} %param.18) | copy-start | bytes 9220
  285.6 282.2 %copy-start.1 = (bf16[63,1536]{1,0:T(8,128)(2,1)S(1)}, bf16[63,1536]{1,0:T(8,128)(2,1)}, u32[]{:S(2)}) copy-start(bf16[63,1536]{1,0:T(8,128)(2,1)} %param.25) | copy-start | bytes 580612
  285.6 282.4 %copy-start.4 = (f32[1536]{0:T(1024)S(1)}, f32[1536]{0:T(1024)}, u32[]{:S(2)}) copy-start(f32[1536]{0:T(1024)} %param.28) | copy-start | bytes 18436
  285.6 281.5 %all-gather.17.cloned.1.call-start = ((), (), s32[]{:S(2)}) async-start(), calls=%async_computation.8 | async-start | bytes 3151872 | tf_op jit(solution)/shard_map/all_gather | solution.py:79
  453.8 154.9 %all-gather.11.cloned.1.call-start = ((), (), s32[]{:S(2)}) async-start(), calls=%async_computation.5 | async-start | bytes 2506752 | tf_op jit(solution)/shard_map/all_gather | solution.py:44
  454.4 197.5 %all-gather.13.cloned.1.call-start = ((), (), s32[]{:S(2)}) async-start(), calls=%async_computation.6 | async-start | bytes 2506752 | tf_op jit(solution)/shard_map/all_gather | solution.py:45
  454.9 240.4 %all-gather.9.cloned.1.call-start = ((), (), s32[]{:S(2)}) async-start(), calls=%async_computation.4 | async-start | bytes 2506752 | tf_op jit(solution)/shard_map/all_gather | solution.py:43
  569.8 46.8 %all-to-all-start.1 = ((bf16[32,16,1536]{2,1,0:T(8,128)(2,1)}), bf16[32,16,1536]{2,1,0:T(8,128)(2,1)S(1)}, u32[]{:S(2)}, u32[]{:S(2)}) async-start(bf16[32,16,1536]{2,1,0:T(8,128)(2,1)} %bitcast.5), calls=%async_computation.1 | async-start | bytes 3145728 | tf_op jit(solution)/shard_map/all_to_all | solution.py:114
  702.1 10.3 %copy-start.5 = (f32[64,4]{0,1:T(4,128)S(1)}, f32[64,4]{0,1:T(4,128)}, u32[]{:S(2)}) copy-start(f32[64,4]{0,1:T(4,128)} %param.27) | copy-start | bytes 3076
  702.1 49.7 %all-to-all-start.2 = ((bf16[32,16,1536]{2,1,0:T(8,128)(2,1)}), bf16[32,16,1536]{2,1,0:T(8,128)(2,1)S(1)}, u32[]{:S(2)}, u32[]{:S(2)}) async-start(bf16[32,16,1536]{2,1,0:T(8,128)(2,1)} %bitcast.10), calls=%async_computation.2 | async-start | bytes 3145728 | tf_op jit(solution)/shard_map/all_to_all | solution.py:121
  754.8 0.7 copy-start.2
Sparse Core Ops, SparseCore 0:
  12.2 121.8 all-gather.14
  285.8 150.9 all-reduce.1
  453.9 113.1 all-gather.16
  569.1 39.4 all-gather.10
  610.6 41.2 all-gather.12
  653.8 41.4 all-gather.8
where the time goes:
time: 763 us; the launch traced here: 762 us
  blocking collectives  423 us (55%)
  waiting for transfers between devices  277 us (36%)
  starting transfers between devices  17.3 us (2%)
  between operations  16.4 us (2%)
  matrix products  14.7 us (2%)
  local copies, waits for them, and re-layouts  7.97 us (1%)
    pmax x1, blocking collectives, on_device(): peak = lax.pmax(local_peak, 'tp')  138 us
    psum x1, blocking collectives, on_device(): weight_total, mixed_sum = lax.psum((local_total, local_mixed), 'tp')  138 us
    all_gather x1, blocking collectives, on_device(): lax.all_gather(new_key_value, ('dp', 'tp'), axis=0, tiled=True)  132 us
    all_gather x1, waiting for transfers between devices, on_device(): all_proj = lax.all_gather(cache_row, ('dp', 'tp'), axis=0, tiled=True)  107 us
    all_gather x1, waiting for transfers between devices, on_device(): lax.all_gather(w_gate, 'dp', axis=1, tiled=True)  43.5 us
    all_to_all x1, waiting for transfers between devices, on_device(): lax.all_to_all(expert_out, 'tp', split_axis=0, concat_axis=0, tiled=True)  39.2 us
    all_gather x1, waiting for transfers between devices, on_device(): lax.all_gather(w_down, 'dp', axis=1, tiled=True)  32.1 us
    all_gather x1, waiting for transfers between devices, on_device(): lax.all_gather(w_up, 'dp', axis=1, tiled=True)  31.7 us
  transfers between devices with their start and end apart: 8, of which 7 were waited for; matrix products, arithmetic and copies ran while one was open for 1% of the time, Pallas kernels for 0%

commit v1 on v0

--- a/solution.py
+++ b/solution.py
@@ -4,6 +4,26 @@
 from jax.sharding import PartitionSpec as P
 
 HIGHEST = lax.Precision.HIGHEST
+
+
+def ratios_map(local_values):
+    group_axis = "dp"
+    slots = lax.axis_size(group_axis)
+    trail = [(b, (b + 1) % slots) for b in range(slots)]
+    field_out, r2 = ([local_values], [local_values])
+    lanes = [(b, (b - 1) % slots) for b in range(slots)]
+    for _ in range(slots // 2):
+        field_out.append(lax.ppermute(field_out[-1], group_axis, trail))
+    pp = 0
+    while pp < (slots - 1) // 2:
+        r2.append(lax.ppermute(r2[-1], group_axis, lanes))
+        pp = pp + 1
+    h_now = jnp.roll(
+        jnp.concatenate([*field_out[::-1], *r2[1:]], 1),
+        (lax.axis_index(group_axis) - slots // 2) * local_values.shape[1],
+        1,
+    )
+    return h_now
 
 
 def contract_rows(left_rows, unit_rows):
@@ -42,7 +62,7 @@
     fetched = (
         lax.all_gather(w_gate, "dp", axis=1, tiled=True),
         lax.all_gather(w_up, "dp", axis=1, tiled=True),
-        lax.all_gather(w_down, "dp", axis=1, tiled=True),
+        ratios_map(w_down),
     )
     all_query, all_new = (
         lax.all_gather(q_new, ("dp", "tp"), axis=0, tiled=True),

time: 763 us -> 723 us (0.948)
  waiting for transfers between devices: 277 us -> 187 us
  local copies, waits for them, and re-layouts: 7.97 us -> 32.6 us
  starting transfers between devices: 17.3 us -> 38 us
    all_gather x1, waiting for transfers between devices: 107 us -> 53.7 us  [on_device(): all_proj = lax.all_gather(cache_row, ('dp', 'tp'), axis=0, tiled=True)]
    all_gather x1 -> x0, waiting for transfers between devices: 32.1 us -> none  [on_device(): lax.all_gather(w_down, 'dp', axis=1, tiled=True)]
    unnamed x28 -> x61, local copies, waits for them, and re-layouts: 3.28 us -> 26.4 us
    ppermute x0 -> x15, starting transfers between devices: none -> 20.9 us  [the longest x7 20.9 us: ratios_map(): r2.append(lax.ppermute(r2[-1], group_axis, lanes))]
    ppermute x0 -> x15, waiting for transfers between devices: none -> 20.6 us  [the longest x8 20.6 us: ratios_map(): field_out.append(lax.ppermute(field_out[-1], group_axis, trail))]
    all_gather x1, waiting for transfers between devices: 43.5 us -> 30.9 us  [on_device(): lax.all_gather(w_gate, 'dp', axis=1, tiled=True)]
    all_gather x1, waiting for transfers between devices: 31.7 us -> 19.6 us  [on_device(): lax.all_gather(w_up, 'dp', axis=1, tiled=True)]
  transfers between devices with their start and end apart: 8 -> 22, of which waited for: 7 -> 14; matrix products, arithmetic and copies ran while one was open for 1% -> 5% of each run, Pallas kernels for 0% -> 0%
where the time goes in v1:
time: 723 us; the launch traced here: 722 us
  blocking collectives  423 us (59%)
  waiting for transfers between devices  187 us (26%)
  starting transfers between devices  38 us (5%)
  local copies, waits for them, and re-layouts  32.6 us (5%)
  matrix products  18.6 us (3%)
  between operations  16.1 us (2%)
  other arithmetic  7.54 us (1%)
    pmax x1, blocking collectives, on_device(): peak = lax.pmax(local_peak, 'tp')  138 us
    psum x1, blocking collectives, on_device(): weight_total, mixed_sum = lax.psum((local_total, local_mixed), 'tp')  138 us
    all_gather x1, blocking collectives, on_device(): lax.all_gather(new_key_value, ('dp', 'tp'), axis=0, tiled=True)  132 us
    all_gather x1, waiting for transfers between devices, on_device(): all_proj = lax.all_gather(cache_row, ('dp', 'tp'), axis=0, tiled=True)  53.7 us
    all_to_all x1, waiting for transfers between devices, on_device(): lax.all_to_all(expert_out, 'tp', split_axis=0, concat_axis=0, tiled=True)  39.2 us
    all_gather x1, waiting for transfers between devices, on_device(): lax.all_gather(w_gate, 'dp', axis=1, tiled=True)  30.9 us
    unnamed x61, local copies, waits for them, and re-layouts  26.4 us
    ppermute x7, starting transfers between devices, ratios_map(): r2.append(lax.ppermute(r2[-1], group_axis, lanes))  20.9 us
  transfers between devices with their start and end apart: 22, of which 14 were waited for; matrix products, arithmetic and copies ran while one was open for 5% of the time, Pallas kernels for 0%

profile of v1, /device:TPU:4, one launch (start us, length us, event | category | flops | bytes accessed | tf_op | source)
XLA Modules:
  0.0 722.2 jit_solution(16123469640966443627)
XLA Ops:
  8.0 132.2 %all-gather.1 = bf16[512,1,512]{2,1,0:T(2,128)(2,1)S(1)} all-gather(bf16[1,1,512]{2,1,0:T(2,128)(2,1)} %bitcast.66), channel_id=1, replica_groups=mesh['dp'=16,'tp'=32] {'dp','tp'}, dimensions={0}, use_global_device_ids=true | all-gather | bytes 525312 | tf_op jit(solution)/shard_map/all_gather | solution.py:69
  147.8 138.1 %pmax.7 = f32[32,2,6]{2,1,0:T(2,128)S(1)} all-reduce(f32[32,2,6]{2,1,0:T(2,128)S(1)} %get-tuple-element.10), channel_id=1, replica_groups=mesh['dp'=16,'tp'=32] {'tp'}, use_global_device_ids=true, to_apply=%region_1.2 | all-reduce | flops 384 | bytes 3072 | tf_op jit(solution)/shard_map/pmax | solution.py:89
  286.0 3.0 fusion.10
  289.3 137.7 %psum.15 = f32[32,2,6]{2,1,0:T(2,128)S(1)} all-reduce(f32[32,2,6]{2,1,0:T(2,128)S(1)} %fusion.24), channel_id=1, replica_groups=mesh['dp'=16,'tp'=32] {'tp'}, use_global_device_ids=true, to_apply=%region_4.5 | all-reduce | flops 384 | bytes 3072 | tf_op jit(solution)/shard_map/psum | solution.py:93
  427.1 13.1 %all-reduce.2.cloned.1.call-done = f32[32,2,6,128]{3,2,1,0:T(8,128)} async-done(((f32[32,2,6,128]{3,2,1,0:T(8,128)}), f32[32,2,6,128]{3,2,1,0:T(8,128)}) %all-reduce.2.cloned.1.call-update) | async-done | bytes 196624 | tf_op jit(solution)/shard_map/psum | solution.py:93
  441.6 14.8 %all_to_all.26 = bf16[32,1,48]{2,1,0:T(2,128)(2,1)S(1)} all-to-all(bf16[32,1,48]{2,1,0:T(2,128)(2,1)S(1)} %copy.45), channel_id=1, replica_groups=mesh['dp'=16,'tp'=32] {'tp'}, dimensions={0} | all-to-all | bytes 6144 | tf_op jit(solution)/shard_map/all_to_all | solution.py:98
  457.8 5.8 collective-permute-done
  463.6 3.0 collective-permute-start.8
  469.4 3.0 collective-permute-start.9
  472.3 2.8 collective-permute-done.2
  475.4 3.0 collective-permute-start.10
  481.6 3.0 collective-permute-start.11
  487.4 3.0 collective-permute-start.12
  493.1 3.0 collective-permute-start.13
  501.1 3.0 collective-permute-start.14
  516.8 53.7 %all-gather.14.cloned.1.call-done = bf16[512,1,1536]{2,1,0:T(2,128)(2,1)} async-done(((bf16[1,1,1536]{2,1,0:T(2,128)(2,1)}), bf16[512,1,1536]{2,1,0:T(2,128)(2,1)}) %all-gather.14.cloned.1.call-update) | async-done | bytes 1572880 | tf_op jit(solution)/shard_map/all_gather | solution.py:99
  573.2 7.1 all-to-all-start.1
  592.4 19.6 %all-gather.10.cloned.1.call-done = bf16[1,768,1536]{2,1,0:T(8,128)(2,1)} async-done(((bf16[1,48,1536]{2,1,0:T(8,128)(2,1)}), bf16[1,768,1536]{2,1,0:T(8,128)(2,1)}) %all-gather.10.cloned.1.call-update) | async-done | bytes 2359312 | tf_op jit(solution)/shard_map/all_gather | solution.py:64
  612.0 8.0 %all-to-all-done.1 = bf16[32,16,1536]{2,1,0:T(8,128)(2,1)S(1)} async-done(((bf16[32,16,1536]{2,1,0:T(8,128)(2,1)}), bf16[32,16,1536]{2,1,0:T(8,128)(2,1)S(1)}, u32[]{:S(2)}, u32[]{:S(2)}) %all-to-all-start.1) | async-done | bytes 1572896 | tf_op jit(solution)/shard_map/all_to_all | solution.py:134
  620.0 4.3 fusion.1
  624.3 30.9 %all-gather.8.cloned.1.call-done = bf16[1,768,1536]{2,1,0:T(8,128)(2,1)} async-done(((bf16[1,48,1536]{2,1,0:T(8,128)(2,1)}), bf16[1,768,1536]{2,1,0:T(8,128)(2,1)}) %all-gather.8.cloned.1.call-update) | async-done | bytes 2359312 | tf_op jit(solution)/shard_map/all_gather | solution.py:63
  655.2 7.2 convolution_convert_fusion
  662.4 9.9 %all-to-all-start.2 = ((bf16[32,16,1536]{2,1,0:T(8,128)(2,1)}), bf16[32,16,1536]{2,1,0:T(8,128)(2,1)S(1)}, u32[]{:S(2)}, u32[]{:S(2)}) async-start(bf16[32,16,1536]{2,1,0:T(8,128)(2,1)} %bitcast.10), calls=%async_computation.2 | async-start | bytes 3145728 | tf_op jit(solution)/shard_map/all_to_all | solution.py:141
  672.8 39.2 %all-to-all-done.2 = bf16[32,16,1536]{2,1,0:T(8,128)(2,1)S(1)} async-done(((bf16[32,16,1536]{2,1,0:T(8,128)(2,1)}), bf16[32,16,1536]{2,1,0:T(8,128)(2,1)S(1)}, u32[]{:S(2)}, u32[]{:S(2)}) %all-to-all-start.2) | async-done | bytes 1572896 | tf_op jit(solution)/shard_map/all_to_all | solution.py:141
  (143 shorter events, 57.8 us)
Async XLA Ops:
  7.2 434.2 %copy-start = (bf16[1536,48]{0,1:T(8,128)(2,1)S(1)}, bf16[1536,48]{0,1:T(8,128)(2,1)}, u32[]{:S(2)}) copy-start(bf16[1536,48]{0,1:T(8,128)(2,1)} %param.24) | copy-start | bytes 442372
  7.2 135.5 %all-gather.12.cloned.1.call-start = ((), (), s32[]{:S(2)}) async-start(), calls=%async_computation.6 | async-start | bytes 3151872 | tf_op jit(solution)/shard_map/all_gather | solution.py:68
  7.9 432.3 %all-reduce.2.cloned.1.call-start = ((), (), s32[]{:S(2)}) async-start(), calls=%async_computation.3 | async-start | bytes 524288 | tf_op jit(solution)/shard_map/psum | solution.py:93
  144.9 353.4 %copy-start.11 = (s32[512]{0:T(512)S(1)}, s32[512]{0:T(512)}, u32[]{:S(2)}) copy-start(s32[512]{0:T(512)} %param.19) | copy-start | bytes 6148
  289.0 281.5 %all-gather.14.cloned.1.call-start = ((), (), s32[]{:S(2)}) async-start(), calls=%async_computation.7 | async-start | bytes 3151872 | tf_op jit(solution)/shard_map/all_gather | solution.py:99
  457.1 154.9 %all-gather.10.cloned.1.call-start = ((), (), s32[]{:S(2)}) async-start(), calls=%async_computation.5 | async-start | bytes 2506752 | tf_op jit(solution)/shard_map/all_gather | solution.py:64
  457.7 197.5 %all-gather.8.cloned.1.call-start = ((), (), s32[]{:S(2)}) async-start(), calls=%async_computation.4 | async-start | bytes 2506752 | tf_op jit(solution)/shard_map/all_gather | solution.py:63
  457.8 5.8 collective-permute-start
  463.6 5.8 collective-permute-start.1
  463.6 5.8 collective-permute-start.8
  469.4 5.8 collective-permute-start.2
  469.4 6.0 collective-permute-start.9
  475.2 5.8 collective-permute-start.3
  475.4 6.1 collective-permute-start.10
  480.9 5.8 collective-permute-start.4
  481.6 5.8 collective-permute-start.11
  486.7 5.8 collective-permute-start.5
  487.4 5.7 collective-permute-start.12
  492.5 5.8 collective-permute-start.6
  493.1 8.0 %collective-permute-start.13 = (bf16[1,48,1536]{2,1,0:T(8,128)(2,1)S(1)}, bf16[1,48,1536]{2,1,0:T(8,128)(2,1)S(1)}, u32[]{:S(2)}, u32[]{:S(2)}) collective-permute-start(bf16[1,48,1536]{2,1,0:T(8,128)(2,1)S(1)} %collective-permute-done.12), channel_id=1, source_target_pairs={{0,480},{32,0},{64,32},{96,64},{128,96},{160,128},{192,160},{224,1... | collective-permute-start | bytes 442376 | tf_op jit(solution)/shard_map/ppermute | solution.py:19
  498.3 5.8 collective-permute-start.7
  501.1 13.1 %collective-permute-start.14 = (bf16[1,48,1536]{2,1,0:T(8,128)(2,1)S(1)}, bf16[1,48,1536]{2,1,0:T(8,128)(2,1)S(1)}, u32[]{:S(2)}, u32[]{:S(2)}) collective-permute-start(bf16[1,48,1536]{2,1,0:T(8,128)(2,1)S(1)} %collective-permute-done.13), channel_id=1, source_target_pairs={{0,480},{32,0},{64,32},{96,64},{128,96},{160,128},{192,160},{224,1... | collective-permute-start | bytes 442376 | tf_op jit(solution)/shard_map/ppermute | solution.py:19
  573.2 46.8 %all-to-all-start.1 = ((bf16[32,16,1536]{2,1,0:T(8,128)(2,1)}), bf16[32,16,1536]{2,1,0:T(8,128)(2,1)S(1)}, u32[]{:S(2)}, u32[]{:S(2)}) async-start(bf16[32,16,1536]{2,1,0:T(8,128)(2,1)} %bitcast.5), calls=%async_computation.1 | async-start | bytes 3145728 | tf_op jit(solution)/shard_map/all_to_all | solution.py:134
  662.4 49.6 %all-to-all-start.2 = ((bf16[32,16,1536]{2,1,0:T(8,128)(2,1)}), bf16[32,16,1536]{2,1,0:T(8,128)(2,1)S(1)}, u32[]{:S(2)}, u32[]{:S(2)}) async-start(bf16[32,16,1536]{2,1,0:T(8,128)(2,1)} %bitcast.10), calls=%async_computation.2 | async-start | bytes 3145728 | tf_op jit(solution)/shard_map/all_to_all | solution.py:141
  (11 other events, 1749.2 us)
Sparse Core Ops, SparseCore 0:
  12.2 121.8 all-gather.11
  289.1 150.9 all-reduce.1
  457.3 113.2 all-gather.13
  572.5 39.4 all-gather.9
  614.0 41.2 all-gather.7
